TPU v7x, 1024 devices: a whole 4x4x32 slice. The times are simulated.
1024 devices in a mesh: gx: 4 (over x), gy: 8 (over y, core), gz: 32 (over z).
Axes of the slice: x: 4, y: 4, z: 32, core: 2. Of those that a mesh axis runs over, the one named last changes fastest.
Arguments:
- residual_in: float32 [4, 8, 32, 128, 768], P('gx', 'gy', 'gz'), as said below
- schur: float32 [4, 8, 32, 768, 768], P('gx', 'gy', 'gz'), as said below
- modes: float32 [4, 8, 32, 6, 768], P('gx', 'gy', 'gz'), may hold values from -0.875 to 0.875
- coarse_inv: float32 [4, 8, 192, 192], P('gx', 'gy', 'gz'), as said below
Outputs:
- multipliers: float32 [4, 8, 32, 128, 768], P('gx', 'gy', 'gz')
- residual: float32 [4, 8, 32, 128, 768], P('gx', 'gy', 'gz')
Inputs may be any that keep to these rules, and one draw needn't show every extreme that they name: `residual_in`: each multiplier has the same value on both sides of its face. `schur`: every subdomain's matrix is symmetric positive definite. `coarse_inv`: every coarse block is symmetric positive definite.
All inputs are finite; a program needn't handle non-finite values.
Results may differ from a plain program's by a relative error of at most 0.0003.
Values sent between devices are 32-bit elements; how exact they have to be, the bound alone decides.
A program may use at most 32 MiB of HBM per device.

v0:
```python
import jax
import jax.numpy as jnp
from jax import lax
from jax.sharding import PartitionSpec as P

ITERS = 4


def with_halo(x, sides, width):
    for axis, dim in sides:
        devices, length = (lax.axis_size(axis), x.shape[dim])
        up = [(i, (i + 1) % devices) for i in range(devices)]
        down = [(j, i) for i, j in up]
        last = lax.slice_in_dim(x, length - width, length, axis=dim)
        initial = lax.slice_in_dim(x, 0, width, axis=dim)
        before = lax.ppermute(last, axis, up)
        after = lax.ppermute(initial, axis, down)
        x = jnp.concatenate([before, x, after], axis=dim)
    return x


def assemble(values, face):
    parts = []
    pair_x = jnp.stack([values[:, 0:face], values[:, face : 2 * face]])
    ext_x = with_halo(pair_x, (("gx", 0),), 1)
    parts.append(pair_x[0] - ext_x[0])
    parts.append(ext_x[3] - pair_x[1])
    pair_y = jnp.stack([values[:, 2 * face : 3 * face], values[:, 3 * face : 4 * face]])
    ext_y = with_halo(pair_y, (("gy", 0),), 1)
    parts.append(pair_y[0] - ext_y[0])
    parts.append(ext_y[3] - pair_y[1])
    pair_z = jnp.stack([values[:, 4 * face : 5 * face], values[:, 5 * face : 6 * face]])
    ext_z = with_halo(pair_z, (("gz", 0),), 1)
    parts.append(pair_z[0] - ext_z[0])
    parts.append(ext_z[3] - pair_z[1])
    return jnp.concatenate(parts, axis=1)


def global_sums(first, second):
    return lax.psum((first, second), ("gx", "gy", "gz"))


def body(residual_in, schur, modes, coarse_inv):
    resid = residual_in[0, 0, 0]
    matrix = schur[0, 0, 0]
    mode_rows = modes[0, 0, 0]
    coarse_rows = coarse_inv[0, 0]
    face = resid.shape[1] // 6
    sign = jnp.repeat(jnp.array([1.0, -1.0, 1.0, -1.0, 1.0, -1.0], dtype=jnp.float32), face)

    def operate(field):
        u = sign * field
        loads = jnp.einsum("mj,rj->mr", mode_rows, u, precision=lax.Precision.HIGHEST)
        amp = jnp.dot(
            coarse_rows,
            lax.all_gather(loads, "gz", axis=0, tiled=True),
            precision=lax.Precision.HIGHEST,
            preferred_element_type=jnp.float32,
        )
        local = jnp.einsum(
            "rj,ij->ri",
            u,
            matrix,
            precision=lax.Precision.HIGHEST,
            preferred_element_type=jnp.float32,
        )
        coarse_term = jnp.einsum("mr,mj->rj", amp, mode_rows, precision=lax.Precision.HIGHEST)
        values = local + coarse_term
        image = assemble(values, face)
        part_norm = 0.5 * jnp.sum(field * field, axis=1)
        part_curv = 0.5 * jnp.sum(field * image, axis=1)
        norm_sum, curv_sum = global_sums(part_norm, part_curv)
        return (image, norm_sum, curv_sum)

    mult = jnp.zeros_like(resid)
    image, norm_now, curv = operate(resid)
    alpha = norm_now / curv
    direction = resid
    along = image
    for step in range(ITERS):
        mult = mult + alpha[:, None] * direction
        resid = resid - alpha[:, None] * along
        if step + 1 < ITERS:
            image, norm_next, curv = operate(resid)
            ratio = norm_next / norm_now
            alpha = norm_next / (curv - ratio * norm_next / alpha)
            direction = resid + ratio[:, None] * direction
            along = image + ratio[:, None] * along
            norm_now = norm_next
    return (mult[None, None, None], resid[None, None, None])


def solution(mesh):
    return jax.shard_map(
        body,
        mesh=mesh,
        in_specs=(
            P("gx", "gy", "gz", None, None),
            P("gx", "gy", "gz", None, None),
            P("gx", "gy", "gz", None, None),
            P("gx", "gy", "gz", None),
        ),
        out_specs=(P("gx", "gy", "gz", None, None), P("gx", "gy", "gz", None, None)),
        check_vma=False,
    )
```

profile of v0, /device:TPU:1, one launch (start us, length us, event | category | flops | bytes accessed | tf_op | source)
XLA Modules:
  0.0 1007.8 jit_solution(16708925571928018918)
XLA Ops:
  1.5 1.4 convolution_bitcast_fusion.3
  2.9 55.5 %all-gather = f32[32,6,128]{2,1,0:T(8,128)S(1)} all-gather(f32[1,6,128]{2,1,0:T(8,128)S(1)} %convolution_bitcast_fusion.3), channel_id=1, replica_groups=mesh['gx'=4,'gy'=8,'gz'=32] {'gz'}, dimensions={0}, use_global_device_ids=true | all-gather | bytes 101376 | tf_op jit(solution)/shard_map/all_gather | solution.py:56
  58.5 3.5 fusion.6
  62.8 3.1 collective-permute-start
  65.9 3.1 collective-permute-done
  69.0 3.2 collective-permute-start.1
  72.2 1.8 collective-permute-done.1
  74.0 18.1 %collective-permute-start.2 = (f32[1,128,128]{2,1,0:T(8,128)S(1)}, f32[1,128,128]{2,1,0:T(8,128)S(1)}, u32[]{:S(2)}, u32[]{:S(2)}) collective-permute-start(f32[1,128,128]{2,1,0:T(8,128)S(1)} %get-tuple-element.55), channel_id=1, source_target_pairs={{0,32},{32,64},{64,96},{96,128},{128,160},{160,192},{192,224},{224... | collective-permute-start | bytes 196616 | tf_op jit(solution)/shard_map/ppermute | solution.py:16
  92.2 1.3 collective-permute-done.2
  93.5 2.4 collective-permute-start.3
  95.9 1.9 collective-permute-done.3
  97.8 1.9 collective-permute-start.4
  99.8 4.9 collective-permute-done.4
  104.7 1.9 collective-permute-start.5
  106.6 3.1 collective-permute-done.5
  111.0 154.3 %all-reduce.3 = (f32[128]{0:T(128)}, f32[128]{0:T(128)}) all-reduce(f32[128]{0:T(128)} %get-tuple-element.59, f32[128]{0:T(128)S(1)} %get-tuple-element.58), channel_id=1, replica_groups=mesh['gx'=4,'gy'=8,'gz'=32] {'gx','gy','gz'}, use_global_device_ids=true, to_apply=%region_1.0 | all-reduce | flops 256 | bytes 2048 | tf_op jit(solution)/shard_map/psum | solution.py:40
  266.0 1.5 constant_dynamic-update-slice_fusion.6
  267.5 1.1 multiply_subtract_fusion.5
  268.6 1.1 convolution_bitcast_fusion.2
  269.7 3.3 fusion.4
  273.0 44.1 %all-gather.1 = f32[32,6,128]{2,1,0:T(8,128)} all-gather(f32[1,6,128]{2,1,0:T(8,128)S(1)} %convolution_bitcast_fusion.2), channel_id=1, replica_groups=mesh['gx'=4,'gy'=8,'gz'=32] {'gz'}, dimensions={0}, use_global_device_ids=true | all-gather | bytes 101376 | tf_op jit(solution)/shard_map/all_gather | solution.py:56
  317.1 1.6 reshape.940
  319.7 1.6 convolution_add_fusion.2
  321.4 1.9 collective-permute-start.6
  323.3 2.0 collective-permute-start.11
  325.3 4.6 collective-permute-start.7
  329.9 16.1 %collective-permute-start.9 = (f32[1,128,128]{2,1,0:T(8,128)S(1)}, f32[1,128,128]{2,1,0:T(8,128)S(1)}, u32[]{:S(2)}, u32[]{:S(2)}) collective-permute-start(f32[1,128,128]{2,1,0:T(8,128)S(1)} %get-tuple-element.44), channel_id=1, source_target_pairs={{32,0},{64,32},{96,64},{128,96},{160,128},{192,160},{224,192},{0,2... | collective-permute-start | bytes 196616 | tf_op jit(solution)/shard_map/ppermute | solution.py:17
  346.0 3.0 collective-permute-start.10
  349.1 1.3 collective-permute-done.8
  350.5 2.3 collective-permute-done.10
  355.0 150.8 %all-reduce.2 = (f32[128]{0:T(128)S(1)}, f32[128]{0:T(128)S(1)}) all-reduce(f32[128]{0:T(128)S(1)} %broadcast_multiply_fusion.5, f32[128]{0:T(128)S(1)} %broadcast_multiply_fusion.4), channel_id=1, replica_groups=mesh['gx'=4,'gy'=8,'gz'=32] {'gx','gy','gz'}, use_global_device_ids=true, to_apply=%region_5.0 | all-reduce | flops 256 | bytes 2048 | tf_op jit(solution)/shard_map/psum | solution.py:40
  505.8 1.2 fusion.63
  513.0 1.1 multiply_subtract_fusion.3
  514.2 1.1 convolution_bitcast_fusion.1
  515.3 3.3 fusion.2
  518.6 44.1 %all-gather.2 = f32[32,6,128]{2,1,0:T(8,128)} all-gather(f32[1,6,128]{2,1,0:T(8,128)S(1)} %convolution_bitcast_fusion.1), channel_id=1, replica_groups=mesh['gx'=4,'gy'=8,'gz'=32] {'gz'}, dimensions={0}, use_global_device_ids=true | all-gather | bytes 101376 | tf_op jit(solution)/shard_map/all_gather | solution.py:56
  562.7 1.6 reshape.942
  564.3 1.2 fusion.52
  565.5 1.6 convolution_add_fusion.1
  567.1 3.2 collective-permute-start.12
  570.3 2.6 collective-permute-start.17
  572.9 3.8 collective-permute-start.13
  576.7 14.8 %collective-permute-start.15 = (f32[1,128,128]{2,1,0:T(8,128)S(1)}, f32[1,128,128]{2,1,0:T(8,128)S(1)}, u32[]{:S(2)}, u32[]{:S(2)}) collective-permute-start(f32[1,128,128]{2,1,0:T(8,128)S(1)} %get-tuple-element.38), channel_id=1, source_target_pairs={{32,0},{64,32},{96,64},{128,96},{160,128},{192,160},{224,192},{0,2... | collective-permute-start | bytes 196616 | tf_op jit(solution)/shard_map/ppermute | solution.py:17
  591.5 3.1 collective-permute-start.16
  594.7 1.4 collective-permute-start.14
  596.1 1.3 collective-permute-done.14
  599.0 1.6 multiply_reduce_fusion.2
  601.6 152.4 %all-reduce.1 = (f32[128]{0:T(128)}, f32[128]{0:T(128)}) all-reduce(f32[128]{0:T(128)} %broadcast_multiply_fusion.3, f32[128]{0:T(128)} %broadcast_multiply_fusion.2), channel_id=1, replica_groups=mesh['gx'=4,'gy'=8,'gz'=32] {'gx','gy','gz'}, use_global_device_ids=true, to_apply=%region_9.0 | all-reduce | flops 256 | bytes 2048 | tf_op jit(solution)/shard_map/psum | solution.py:40
  754.0 1.3 fusion.62
  760.6 1.3 multiply_add_fusion.1
  762.6 3.3 fusion
  765.9 44.8 %all-gather.3 = f32[32,6,128]{2,1,0:T(8,128)} all-gather(f32[1,6,128]{2,1,0:T(8,128)S(1)} %convolution_bitcast_fusion), channel_id=1, replica_groups=mesh['gx'=4,'gy'=8,'gz'=32] {'gz'}, dimensions={0}, use_global_device_ids=true | all-gather | bytes 101376 | tf_op jit(solution)/shard_map/all_gather | solution.py:56
  810.8 1.6 reshape.944
  812.4 1.2 fusion.50
  813.5 1.6 convolution_add_fusion
  815.2 2.7 collective-permute-start.18
  817.9 1.9 collective-permute-start.23
  819.8 4.0 collective-permute-start.19
  823.8 15.1 %collective-permute-start.21 = (f32[1,128,128]{2,1,0:T(8,128)S(1)}, f32[1,128,128]{2,1,0:T(8,128)S(1)}, u32[]{:S(2)}, u32[]{:S(2)}) collective-permute-start(f32[1,128,128]{2,1,0:T(8,128)S(1)} %get-tuple-element.32), channel_id=1, source_target_pairs={{32,0},{64,32},{96,64},{128,96},{160,128},{192,160},{224,192},{0,2... | collective-permute-start | bytes 196616 | tf_op jit(solution)/shard_map/ppermute | solution.py:17
  838.9 3.5 collective-permute-start.22
  843.2 1.3 collective-permute-done.20
  844.6 1.1 collective-permute-done.22
  848.3 151.2 %all-reduce = (f32[128]{0:T(128)}, f32[128]{0:T(128)}) all-reduce(f32[128]{0:T(128)} %broadcast_multiply_fusion.1, f32[128]{0:T(128)} %broadcast_multiply_fusion), channel_id=1, replica_groups=mesh['gx'=4,'gy'=8,'gz'=32] {'gx','gy','gz'}, use_global_device_ids=true, to_apply=%region_13.0 | all-reduce | flops 256 | bytes 2048 | tf_op jit(solution)/shard_map/psum | solution.py:40
  1005.5 2.2 multiply_subtract_fusion
  (182 shorter events, 31.2 us)
Async XLA Ops:
  0.6 57.8 %copy-start = (f32[1,1,1,768,768]{4,3,2,1,0:T(8,128)S(1)}, f32[1,1,1,768,768]{4,3,2,1,0:T(8,128)}, u32[]{:S(2)}) copy-start(f32[1,1,1,768,768]{4,3,2,1,0:T(8,128)} %param.6) | copy-start | bytes 7077892
  0.6 61.5 %copy-start.13 = (f32[1,1,1,6,768]{4,2,3,1,0:T(1,128)S(1)}, f32[1,1,1,6,768]{4,2,3,1,0:T(1,128)}, u32[]{:S(2)}) copy-start(f32[1,1,1,6,768]{4,2,3,1,0:T(1,128)} %param.7) | copy-start | bytes 55300
  0.7 61.3 %copy-start.39 = (f32[1,1,6,192]{3,1,2,0:T(1,128)S(1)}, f32[1,1,6,192]{3,1,2,0:T(1,128)}, u32[]{:S(2)}) copy-start(f32[1,1,6,192]{3,1,2,0:T(1,128)} %param.8) | copy-start | bytes 13828
  62.0 48.3 %copy-start.1 = (f32[1,1,1,128,768]{4,3,2,1,0:T(8,128)S(1)}, f32[1,1,1,128,768]{4,3,2,1,0:T(8,128)}, u32[]{:S(2)}) copy-start(f32[1,1,1,128,768]{4,3,2,1,0:T(8,128)} %param.5) | copy-start | bytes 1179652
  62.8 6.2 collective-permute-start
  69.0 5.0 collective-permute-start.1
  74.0 19.4 %collective-permute-start.2 = (f32[1,128,128]{2,1,0:T(8,128)S(1)}, f32[1,128,128]{2,1,0:T(8,128)S(1)}, u32[]{:S(2)}, u32[]{:S(2)}) collective-permute-start(f32[1,128,128]{2,1,0:T(8,128)S(1)} %get-tuple-element.55), channel_id=1, source_target_pairs={{0,32},{32,64},{64,96},{96,128},{128,160},{160,192},{192,224},{224... | collective-permute-start | bytes 196616 | tf_op jit(solution)/shard_map/ppermute | solution.py:16
  93.5 4.3 collective-permute-start.3
  97.8 6.8 collective-permute-start.4
  104.7 5.0 collective-permute-start.5
  106.6 3.1 copy-start.12
  110.3 243.7 %copy-start.2 = (f32[128,768]{1,0:T(8,128)}, f32[128,768]{1,0:T(8,128)S(1)}, u32[]{:S(2)}) copy-start(f32[128,768]{1,0:T(8,128)S(1)} %constant_dynamic-update-slice_fusion) | copy-start | bytes 1179652
  266.0 88.0 %copy-start.47 = (f32[128]{0:T(128)}, f32[128]{0:T(128)S(1)}, u32[]{:S(2)}) copy-start(f32[128]{0:T(128)S(1)} %div.30) | copy-start | bytes 1540
  321.3 31.5 %copy-start.8 = (f32[128,768]{1,0:T(8,128)}, f32[128,768]{1,0:T(8,128)S(1)}, u32[]{:S(2)}) copy-start(f32[128,768]{1,0:T(8,128)S(1)} %convolution_add_fusion.2) | copy-start | bytes 1179652
  321.4 27.7 %collective-permute-start.6 = (f32[1,128,128]{2,1,0:T(8,128)S(1)}, f32[1,128,128]{2,1,0:T(8,128)S(1)}, u32[]{:S(2)}, u32[]{:S(2)}) collective-permute-start(f32[1,128,128]{2,1,0:T(8,128)S(1)} %get-tuple-element.47), channel_id=1, source_target_pairs={{0,256},{256,512},{512,768},{768,0},{1,257},{257,513},{513,769},{7... | collective-permute-start | bytes 196616 | tf_op jit(solution)/shard_map/ppermute | solution.py:16
  323.3 29.5 %collective-permute-start.11 = (f32[1,128,128]{2,1,0:T(8,128)S(1)}, f32[1,128,128]{2,1,0:T(8,128)S(1)}, u32[]{:S(2)}, u32[]{:S(2)}) collective-permute-start(f32[1,128,128]{2,1,0:T(8,128)S(1)} %get-tuple-element.42), channel_id=1, source_target_pairs={{1,0},{2,1},{3,2},{4,3},{5,4},{6,5},{7,6},{8,7},{9,8},{10,9},{11,1... | collective-permute-start | bytes 196616 | tf_op jit(solution)/shard_map/ppermute | solution.py:17
  325.3 23.8 %collective-permute-start.7 = (f32[1,128,128]{2,1,0:T(8,128)S(1)}, f32[1,128,128]{2,1,0:T(8,128)S(1)}, u32[]{:S(2)}, u32[]{:S(2)}) collective-permute-start(f32[1,128,128]{2,1,0:T(8,128)S(1)} %get-tuple-element.43), channel_id=1, source_target_pairs={{256,0},{512,256},{768,512},{0,768},{257,1},{513,257},{769,513},{1... | collective-permute-start | bytes 196616 | tf_op jit(solution)/shard_map/ppermute | solution.py:17
  329.9 20.5 %collective-permute-start.9 = (f32[1,128,128]{2,1,0:T(8,128)S(1)}, f32[1,128,128]{2,1,0:T(8,128)S(1)}, u32[]{:S(2)}, u32[]{:S(2)}) collective-permute-start(f32[1,128,128]{2,1,0:T(8,128)S(1)} %get-tuple-element.44), channel_id=1, source_target_pairs={{32,0},{64,32},{96,64},{128,96},{160,128},{192,160},{224,192},{0,2... | collective-permute-start | bytes 196616 | tf_op jit(solution)/shard_map/ppermute | solution.py:17
  346.0 6.8 collective-permute-start.10
  349.0 3.8 copy-start.28
  349.1 1.4 collective-permute-start.8
  349.1 3.7 copy-start.34
  350.4 2.4 copy-start.37
  350.4 2.4 copy-start.32
  354.1 0.9 copy-start.9
  505.8 6.5 copy-start.48
  507.0 7.2 copy-start.43
  564.3 34.7 %copy-start.3 = (f32[128,768]{1,0:T(8,128)S(1)}, f32[128,768]{1,0:T(8,128)}, u32[]{:S(2)}) copy-start(f32[128,768]{1,0:T(8,128)} %copy-done.2) | copy-start | bytes 1179652
  564.3 34.7 %copy-start.10 = (f32[128,768]{1,0:T(8,128)S(1)}, f32[128,768]{1,0:T(8,128)}, u32[]{:S(2)}) copy-start(f32[128,768]{1,0:T(8,128)} %copy-done.9) | copy-start | bytes 1179652
  564.3 34.7 %copy-start.19 = (f32[128,768]{1,0:T(8,128)S(1)}, f32[128,768]{1,0:T(8,128)}, u32[]{:S(2)}) copy-start(f32[128,768]{1,0:T(8,128)} %get-tuple-element.27) | copy-start | bytes 1179652
  567.0 31.3 %copy-start.7 = (f32[128,768]{1,0:T(8,128)}, f32[128,768]{1,0:T(8,128)S(1)}, u32[]{:S(2)}) copy-start(f32[128,768]{1,0:T(8,128)S(1)} %convolution_add_fusion.1) | copy-start | bytes 1179652
  567.1 27.5 %collective-permute-start.12 = (f32[1,128,128]{2,1,0:T(8,128)S(1)}, f32[1,128,128]{2,1,0:T(8,128)S(1)}, u32[]{:S(2)}, u32[]{:S(2)}) collective-permute-start(f32[1,128,128]{2,1,0:T(8,128)S(1)} %get-tuple-element.41), channel_id=1, source_target_pairs={{0,256},{256,512},{512,768},{768,0},{1,257},{257,513},{513,769},{7... | collective-permute-start | bytes 196616 | tf_op jit(solution)/shard_map/ppermute | solution.py:16
  570.3 28.0 %collective-permute-start.17 = (f32[1,128,128]{2,1,0:T(8,128)S(1)}, f32[1,128,128]{2,1,0:T(8,128)S(1)}, u32[]{:S(2)}, u32[]{:S(2)}) collective-permute-start(f32[1,128,128]{2,1,0:T(8,128)S(1)} %get-tuple-element.36), channel_id=1, source_target_pairs={{1,0},{2,1},{3,2},{4,3},{5,4},{6,5},{7,6},{8,7},{9,8},{10,9},{11,1... | collective-permute-start | bytes 196616 | tf_op jit(solution)/shard_map/ppermute | solution.py:17
  572.9 23.1 %collective-permute-start.13 = (f32[1,128,128]{2,1,0:T(8,128)S(1)}, f32[1,128,128]{2,1,0:T(8,128)S(1)}, u32[]{:S(2)}, u32[]{:S(2)}) collective-permute-start(f32[1,128,128]{2,1,0:T(8,128)S(1)} %get-tuple-element.37), channel_id=1, source_target_pairs={{256,0},{512,256},{768,512},{0,768},{257,1},{513,257},{769,513},{1... | collective-permute-start | bytes 196616 | tf_op jit(solution)/shard_map/ppermute | solution.py:17
  576.7 20.7 %collective-permute-start.15 = (f32[1,128,128]{2,1,0:T(8,128)S(1)}, f32[1,128,128]{2,1,0:T(8,128)S(1)}, u32[]{:S(2)}, u32[]{:S(2)}) collective-permute-start(f32[1,128,128]{2,1,0:T(8,128)S(1)} %get-tuple-element.38), channel_id=1, source_target_pairs={{32,0},{64,32},{96,64},{128,96},{160,128},{192,160},{224,192},{0,2... | collective-permute-start | bytes 196616 | tf_op jit(solution)/shard_map/ppermute | solution.py:17
  591.5 6.8 collective-permute-start.16
  594.6 3.7 copy-start.24
  594.7 2.7 collective-permute-start.14
  596.1 2.3 copy-start.31
  597.4 1.0 copy-start.36
  597.4 1.0 copy-start.29
  598.9 1.6 copy-start.15
  754.0 7.9 copy-start.14
  755.3 6.6 copy-start.45
  755.3 10.6 %copy-start.40 = (f32[128]{0:T(128)}, f32[128]{0:T(128)S(1)}, u32[]{:S(2)}) copy-start(f32[128]{0:T(128)S(1)} %get-tuple-element.20) | copy-start | bytes 1540
  812.3 34.0 %copy-start.4 = (f32[128,768]{1,0:T(8,128)S(1)}, f32[128,768]{1,0:T(8,128)}, u32[]{:S(2)}) copy-start(f32[128,768]{1,0:T(8,128)} %copy-done.2) | copy-start | bytes 1179652
  812.3 34.0 %copy-start.11 = (f32[128,768]{1,0:T(8,128)S(1)}, f32[128,768]{1,0:T(8,128)}, u32[]{:S(2)}) copy-start(f32[128,768]{1,0:T(8,128)} %copy-done.9) | copy-start | bytes 1179652
  812.3 34.0 %copy-start.16 = (f32[128,768]{1,0:T(8,128)S(1)}, f32[128,768]{1,0:T(8,128)}, u32[]{:S(2)}) copy-start(f32[128,768]{1,0:T(8,128)} %copy-done.15) | copy-start | bytes 1179652
  812.3 34.0 %copy-start.18 = (f32[128,768]{1,0:T(8,128)S(1)}, f32[128,768]{1,0:T(8,128)}, u32[]{:S(2)}) copy-start(f32[128,768]{1,0:T(8,128)} %get-tuple-element.23) | copy-start | bytes 1179652
  812.4 34.0 %copy-start.41 = (f32[128]{0:T(128)S(1)}, f32[128]{0:T(128)}, u32[]{:S(2)}) copy-start(f32[128]{0:T(128)} %copy-done.40) | copy-start | bytes 1540
  815.1 30.6 %copy-start.6 = (f32[128,768]{1,0:T(8,128)}, f32[128,768]{1,0:T(8,128)S(1)}, u32[]{:S(2)}) copy-start(f32[128,768]{1,0:T(8,128)S(1)} %convolution_add_fusion) | copy-start | bytes 1179652
  815.2 190.3 %copy-start.42 = (f32[128]{0:T(128)S(1)}, f32[128]{0:T(128)}, u32[]{:S(2)}) copy-start(f32[128]{0:T(128)} %copy-done.40) | copy-start | bytes 1540
  815.2 190.3 %copy-start.44 = (f32[128]{0:T(128)S(1)}, f32[128]{0:T(128)}, u32[]{:S(2)}) copy-start(f32[128]{0:T(128)} %copy-done.43) | copy-start | bytes 1540
  815.2 190.3 %copy-start.46 = (f32[128]{0:T(128)S(1)}, f32[128]{0:T(128)}, u32[]{:S(2)}) copy-start(f32[128]{0:T(128)} %copy-done.45) | copy-start | bytes 1540
  815.2 27.2 %collective-permute-start.18 = (f32[1,128,128]{2,1,0:T(8,128)S(1)}, f32[1,128,128]{2,1,0:T(8,128)S(1)}, u32[]{:S(2)}, u32[]{:S(2)}) collective-permute-start(f32[1,128,128]{2,1,0:T(8,128)S(1)} %get-tuple-element.35), channel_id=1, source_target_pairs={{0,256},{256,512},{512,768},{768,0},{1,257},{257,513},{513,769},{7... | collective-permute-start | bytes 196616 | tf_op jit(solution)/shard_map/ppermute | solution.py:16
  817.9 27.8 %collective-permute-start.23 = (f32[1,128,128]{2,1,0:T(8,128)S(1)}, f32[1,128,128]{2,1,0:T(8,128)S(1)}, u32[]{:S(2)}, u32[]{:S(2)}) collective-permute-start(f32[1,128,128]{2,1,0:T(8,128)S(1)} %get-tuple-element.30), channel_id=1, source_target_pairs={{1,0},{2,1},{3,2},{4,3},{5,4},{6,5},{7,6},{8,7},{9,8},{10,9},{11,1... | collective-permute-start | bytes 196616 | tf_op jit(solution)/shard_map/ppermute | solution.py:17
  819.8 23.4 %collective-permute-start.19 = (f32[1,128,128]{2,1,0:T(8,128)S(1)}, f32[1,128,128]{2,1,0:T(8,128)S(1)}, u32[]{:S(2)}, u32[]{:S(2)}) collective-permute-start(f32[1,128,128]{2,1,0:T(8,128)S(1)} %get-tuple-element.31), channel_id=1, source_target_pairs={{256,0},{512,256},{768,512},{0,768},{257,1},{513,257},{769,513},{1... | collective-permute-start | bytes 196616 | tf_op jit(solution)/shard_map/ppermute | solution.py:17
  823.8 20.8 %collective-permute-start.21 = (f32[1,128,128]{2,1,0:T(8,128)S(1)}, f32[1,128,128]{2,1,0:T(8,128)S(1)}, u32[]{:S(2)}, u32[]{:S(2)}) collective-permute-start(f32[1,128,128]{2,1,0:T(8,128)S(1)} %get-tuple-element.32), channel_id=1, source_target_pairs={{32,0},{64,32},{96,64},{128,96},{160,128},{192,160},{224,192},{0,2... | collective-permute-start | bytes 196616 | tf_op jit(solution)/shard_map/ppermute | solution.py:17
  838.9 6.8 collective-permute-start.22
  842.4 3.4 copy-start.23
  842.4 2.1 collective-permute-start.20
  843.2 2.6 copy-start.27
  844.5 1.3 copy-start.35
  844.5 1.2 copy-start.25
  (9 other events, 5.9 us)
where the time goes:
time: 1010 us
  blocking collectives  797 us (79%)
  starting transfers between devices  115 us (11%)
  other arithmetic  33.4 us (3%)
  matrix products  26.4 us (3%)
  waiting for transfers between devices  24.2 us (2%)
    psum x4, blocking collectives, global_sums(): return lax.psum((first, second), ('gx', 'gy', 'gz'))  609 us
    all_gather x4, blocking collectives, operate(): lax.all_gather(loads, 'gz', axis=0, tiled=True)  189 us
    ppermute x12, starting transfers between devices, with_halo(): after = lax.ppermute(initial, axis, down)  72.4 us
    ppermute x12, starting transfers between devices, with_halo(): before = lax.ppermute(last, axis, up)  42.8 us
  transfers between devices with their start and end apart: 24, of which 12 were waited for; matrix products, arithmetic and copies ran while one was open for 0% of the time, Pallas kernels for 0%

commit v1 on v0

v1 whole, which is shorter than its diff:
```python
import functools

import jax
import jax.numpy as jnp
from jax import lax
from jax.experimental import pallas as pl
from jax.experimental.pallas import tpu as pltpu
from jax.sharding import PartitionSpec as P

MESH = pl.DeviceIdType.MESH
ITERS = 4
FACE = 128
IF = 6 * FACE
LOADS = 128
MODES = 6
SLOT = 8
AUG = IF + 16
F32 = jnp.float32
BF16 = jnp.bfloat16


def gather_plan(nz):
    if nz == 32:
        direct = [13, -13, 7, -7, 3, -3, 2, -2, 1, -1]
        relays = [
            (7, [3, -3, 2, -2, 1, -1]),
            (-7, [-3, 3, -2, 2, -1, 1]),
            (13, [3, -2, 2, -1, 1]),
            (-13, [-2, 2, -1, 1]),
        ]
        return direct, relays
    direct = [1]
    relays = [(1, list(range(1, nz - 1)))]
    return direct, relays


def split(x):
    hi = x.astype(BF16)
    return hi, (x - hi.astype(F32)).astype(BF16)


def mm(a, b):
    return jnp.dot(a, b, preferred_element_type=F32)


def kernel(
    sizes, res_hbm, schur_hbm, modes_hbm, coarse_hbm, mult_ref, out_ref,
    res_v, schur_v, modes_v, coarse_v, modes8, coarse8, cbuf, c_hi, c_lo, pmodes, tcat, m_hi, m_lo, ucat,
    r_buf, p_buf, s_buf, x_buf, y_buf, q_buf, zq_buf, zs_buf,
    gbuf, abuf, acol, xysrc, xybuf, hbuf,
    local_sem, schur_sem, c_send, c_recv, m_send, m_recv, z_send, z_recv, h_send, h_recv, a_send, a_recv, xy_send, xy_recv,
):
    nx, ny, nz = sizes
    mx, my, mz = lax.axis_index("gx"), lax.axis_index("gy"), lax.axis_index("gz")

    def device(dx, dy, dz):
        return (lax.rem(mx + dx % nx, nx), lax.rem(my + dy % ny, ny), lax.rem(mz + dz % nz, nz))

    direct, relays = gather_plan(nz)
    others = [(dx, dy) for dx in range(nx) for dy in range(ny) if dx or dy]

    def far(d):
        dx, dy = d
        return -(min(dx, nx - dx) + min(dy, ny - dy))

    others.sort(key=far)
    faces = [(-1, 0, 0), (1, 0, 0), (0, -1, 0), (0, 1, 0), (0, 0, -1), (0, 0, 1)]

    load_modes = pltpu.make_async_copy(modes_hbm, modes_v, local_sem.at[0])
    load_coarse = pltpu.make_async_copy(coarse_hbm, coarse_v, local_sem.at[1])
    load_res = pltpu.make_async_copy(res_hbm, res_v, local_sem.at[2])
    load_modes.start()
    load_coarse.start()
    load_res.start()
    load_schur = []
    for f in range(6):
        rows = pl.ds(f * FACE, FACE)
        copy = pltpu.make_async_copy(schur_hbm.at[rows], schur_v.at[rows], schur_sem.at[f])
        copy.start()
        load_schur.append(copy)

    barrier = pltpu.get_barrier_semaphore()
    z_targets = sorted(set(o % nz for o in direct) | set(o % nz for _, steps in relays for o in steps))
    z_all = sorted(set(z_targets) | set((-o) % nz for o in z_targets) | {1, nz - 1})
    for dz in z_all:
        pl.semaphore_signal(barrier, inc=1, device_id=device(0, 0, dz), device_id_type=MESH)
    for dx, dy in others:
        pl.semaphore_signal(barrier, inc=1, device_id=device(dx, dy, 0), device_id_type=MESH)

    coarse8[...] = jnp.zeros_like(coarse8)
    modes8[...] = jnp.zeros_like(modes8)
    load_coarse.wait()
    coarse8[0:MODES] = coarse_v[...]
    cn = MODES * nz
    cp = SLOT * nz
    row = lax.broadcasted_iota(jnp.int32, (cn, cp), 0)
    col = lax.broadcasted_iota(jnp.int32, (cn, cp), 1)
    mode = lax.rem(col, SLOT)
    pick = (row == MODES * (col // SLOT) + mode) & (mode < MODES)
    spread = jnp.where(pick, 1.0, 0.0).astype(F32)
    cbuf[mz] = jnp.dot(coarse8[...], spread, precision=lax.Precision.HIGHEST, preferred_element_type=F32)
    load_modes.wait()
    modes8[0:MODES] = modes_v[...]

    def z_copy(buf, send, recv, n, source, step, offset):
        slot = lax.rem(mz + (-source) % nz, nz)
        return pltpu.make_async_remote_copy(
            src_ref=buf.at[slot], dst_ref=buf.at[slot], send_sem=send.at[n], recv_sem=recv.at[offset % nz],
            device_id=device(0, 0, step), device_id_type=MESH,
        )

    def z_arrival(buf, send, recv, offset):
        slot = lax.rem(mz + (-offset) % nz, nz)
        return pltpu.make_async_remote_copy(
            src_ref=buf.at[slot], dst_ref=buf.at[slot], send_sem=send.at[0], recv_sem=recv.at[offset % nz],
            device_id=device(0, 0, 1), device_id_type=MESH,
        )

    def z_first(buf, send, recv):
        return [z_copy(buf, send, recv, n, 0, o, o) for n, o in enumerate(direct)]

    def z_relays(buf, send, recv):
        n, out = len(direct), []
        for centre, steps in relays:
            copies = []
            for step in steps:
                copies.append(z_copy(buf, send, recv, n, centre, step, centre + step))
                n += 1
            out.append((centre, copies))
        return out

    relayed = [centre % nz for centre, _ in relays]
    rest = [o for o in range(1, nz) if o not in relayed]

    def relay(buf, send, recv):
        for centre, copies in z_relays(buf, send, recv):
            z_arrival(buf, send, recv, centre).wait_recv()
            for copy in copies:
                copy.start()

    def finish(buf, send, recv):
        for offset in rest:
            z_arrival(buf, send, recv, offset).wait_recv()

    def sent(buf, send, recv):
        for copy in z_first(buf, send, recv):
            copy.wait_send()
        for _, copies in z_relays(buf, send, recv):
            for copy in copies:
                copy.wait_send()

    pl.semaphore_wait(barrier, len(z_all) + len(others))

    for copy in z_first(cbuf, c_send, c_recv):
        copy.start()

    def mode_copy(f):
        return pltpu.make_async_remote_copy(
            src_ref=modes8.at[:, pl.ds(f * FACE, FACE)], dst_ref=pmodes.at[f ^ 1], send_sem=m_send.at[f], recv_sem=m_recv.at[f ^ 1],
            device_id=device(*faces[f]), device_id_type=MESH,
        )

    for f in range(6):
        mode_copy(f).start()

    def halo_copy(par, f):
        return pltpu.make_async_remote_copy(
            src_ref=y_buf.at[pl.ds(f * FACE, FACE)], dst_ref=hbuf.at[par, f ^ 1], send_sem=h_send.at[f], recv_sem=h_recv.at[par, f ^ 1],
            device_id=device(*faces[f]), device_id_type=MESH,
        )

    def halo_arrival(par, f):
        return pltpu.make_async_remote_copy(
            src_ref=y_buf.at[pl.ds(f * FACE, FACE)], dst_ref=hbuf.at[par, f], send_sem=h_send.at[f], recv_sem=h_recv.at[par, f],
            device_id=device(*faces[f]), device_id_type=MESH,
        )

    def a_copy(par, f):
        return pltpu.make_async_remote_copy(
            src_ref=acol.at[mz], dst_ref=abuf.at[par, f ^ 1], send_sem=a_send.at[f], recv_sem=a_recv.at[par, f ^ 1],
            device_id=device(*faces[f]), device_id_type=MESH,
        )

    def a_arrival(par, f):
        return pltpu.make_async_remote_copy(
            src_ref=acol.at[mz], dst_ref=abuf.at[par, f], send_sem=a_send.at[f], recv_sem=a_recv.at[par, f],
            device_id=device(*faces[f]), device_id_type=MESH,
        )

    my_slot = mx * ny + my

    def xy_copy(par, n):
        dx, dy = others[n]
        return pltpu.make_async_remote_copy(
            src_ref=xysrc, dst_ref=xybuf.at[par, my_slot], send_sem=xy_send.at[n], recv_sem=xy_recv.at[par, n],
            device_id=device(dx, dy, 0), device_id_type=MESH,
        )

    def xy_arrival(par, n):
        dx, dy = others[n]
        from_x, from_y, _ = device(-dx, -dy, 0)
        return pltpu.make_async_remote_copy(
            src_ref=xysrc, dst_ref=xybuf.at[par, from_x * ny + from_y], send_sem=xy_send.at[n], recv_sem=xy_recv.at[par, n],
            device_id=device(dx, dy, 0), device_id_type=MESH,
        )

    def apply_local():
        for lo, size in ((0, 400), (400, 384)):
            rows = slice(lo, lo + size)
            both = mm(m_hi[rows], ucat[...])
            zq_buf[rows] = both[:, :LOADS] + both[:, LOADS:] + mm(m_lo[rows], ucat[:, :LOADS])

    load_res.wait()
    for f in range(6):
        block = jnp.transpose(res_v[:, f * FACE:(f + 1) * FACE])
        if f % 2:
            block = -block
        rows = slice(f * FACE, (f + 1) * FACE)
        r_buf[0, rows] = block
        hi, lo = split(block)
        ucat[rows, :LOADS] = hi
        ucat[rows, LOADS:] = lo
    w_aug = jnp.concatenate([modes8[...], jnp.zeros((8, IF), F32)], axis=0)
    hi, lo = split(w_aug)
    m_hi[IF:AUG] = hi
    m_lo[IF:AUG] = lo
    for f in range(6):
        load_schur[f].wait()
        rows = slice(f * FACE, (f + 1) * FACE)
        hi, lo = split(schur_v[rows])
        m_hi[rows] = hi
        m_lo[rows] = lo
    apply_local()

    def post(par, r_par, first, alpha):
        norm = jnp.zeros((8, LOADS), F32)
        energy = jnp.zeros((8, LOADS), F32)
        for f in range(6):
            rows = slice(f * FACE, (f + 1) * FACE)
            y = zq_buf[rows] if first else y_buf[rows] - alpha * zs_buf[rows]
            y_buf[rows] = y
            r = r_buf[r_par, rows]
            norm = norm + jnp.sum((r * r).reshape(FACE // 8, 8, LOADS), axis=0)
            energy = energy + jnp.sum((r * y).reshape(FACE // 8, 8, LOADS), axis=0)
        rows = slice(IF, IF + SLOT)
        g = zq_buf[rows] if first else y_buf[rows] - alpha * zs_buf[rows]
        y_buf[rows] = g
        gbuf[par, mz] = g
        gbuf[par, mz, MODES:MODES + 1] = jnp.sum(norm, axis=0, keepdims=True)
        gbuf[par, mz, MODES + 1:SLOT] = jnp.sum(energy, axis=0, keepdims=True)

    def launch(par):
        for copy in z_first(gbuf.at[par], z_send, z_recv.at[par]):
            copy.start()
        for f in (4, 5, 0, 1, 2, 3):
            halo_copy(par, f).start()

    post(0, 0, True, None)
    launch(0)

    x_buf[...] = jnp.zeros_like(x_buf)
    p_buf[...] = jnp.zeros_like(p_buf)
    s_buf[...] = jnp.zeros_like(s_buf)
    zs_buf[...] = jnp.zeros_like(zs_buf)
    relay(cbuf, c_send, c_recv)

    for f in range(6):
        mode_copy(f).wait_send()
    for f in range(6):
        pltpu.make_async_remote_copy(
            src_ref=modes8.at[:, pl.ds(f * FACE, FACE)], dst_ref=pmodes.at[f], send_sem=m_send.at[f], recv_sem=m_recv.at[f],
            device_id=device(*faces[f]), device_id_type=MESH,
        ).wait_recv()
    zero8 = jnp.zeros((SLOT, FACE), F32)
    for f in range(6):
        pieces = [zero8] * 8
        pieces[0] = modes8[:, f * FACE:(f + 1) * FACE]
        pieces[1 + f] = -pmodes[f]
        hi, lo = split(jnp.concatenate(pieces, axis=0))
        stack = jnp.concatenate([hi.astype(F32), lo.astype(F32), hi.astype(F32), jnp.zeros((64, FACE), F32)], axis=0)
        tcat[f * FACE:(f + 1) * FACE] = jnp.transpose(stack).astype(BF16)

    def step(k, carry):
        alpha_before, rr = carry
        par = lax.rem(k, 2)
        after = 1 - par
        g_now, recv_now = gbuf.at[par], z_recv.at[par]
        relay(g_now, z_send, recv_now)

        @pl.when(k == 0)
        def _():
            finish(cbuf, c_send, c_recv)
            hi, lo = split(cbuf[...].reshape(cp, cp))
            c_hi[...] = hi
            c_lo[...] = lo
            sent(cbuf, c_send, c_recv)

        finish(g_now, z_send, recv_now)
        g = gbuf[par]
        total = jnp.sum(g, axis=0)
        g = g.reshape(cp, LOADS)
        g_hi, g_lo = split(g)
        both = mm(c_hi[...], jnp.concatenate([g_hi, g_lo], axis=1))
        a = both[:, :LOADS] + both[:, LOADS:] + mm(c_lo[...], g_hi)
        acol[...] = a.reshape(nz, SLOT, LOADS)
        for f in range(4):
            a_copy(par, f).start()
        coarse_energy = jnp.sum(a * g, axis=0, keepdims=True)
        xysrc[0:1] = total[MODES:MODES + 1]
        xysrc[1:2] = total[MODES + 1:SLOT] + coarse_energy
        for n in range(len(others)):
            xy_copy(par, n).start()
        xybuf[par, my_slot] = xysrc[...]

        for f in range(6):
            halo_arrival(par, f).wait_recv()
        for f in range(4):
            a_arrival(par, f).wait_recv()
        pieces = [acol[mz]] + [abuf[par, f] for f in range(4)]
        pieces += [acol[lax.rem(mz + nz - 1, nz)], acol[lax.rem(mz + 1, nz)], jnp.zeros((SLOT, LOADS), F32)]
        hi, lo = split(jnp.concatenate(pieces, axis=0))
        amps = jnp.concatenate([hi, hi, lo, jnp.zeros((64, LOADS), BF16)], axis=0)
        for f in range(6):
            rows = slice(f * FACE, (f + 1) * FACE)
            q = y_buf[rows] - hbuf[par, f] + mm(tcat[rows], amps)
            q_buf[rows] = q
            hi, lo = split(q)
            ucat[rows, :LOADS] = hi
            ucat[rows, LOADS:] = lo

        @pl.when(k < ITERS - 1)
        def _():
            apply_local()

        sent(g_now, z_send, recv_now)
        for f in range(6):
            halo_copy(par, f).wait_send()
        for f in range(4):
            a_copy(par, f).wait_send()
        for n in range(len(others)):
            xy_copy(par, n).wait_send()
        for n in range(len(others)):
            xy_arrival(par, n).wait_recv()
        sums = jnp.sum(xybuf[par], axis=0)
        new = 0.5 * sums[0:1]
        curv = sums[1:2]
        beta = jnp.where(k == 0, jnp.zeros_like(new), new / rr)
        alpha = new / (curv - beta * new / alpha_before)

        for f in range(6):
            rows = slice(f * FACE, (f + 1) * FACE)
            s = q_buf[rows] + beta * s_buf[rows]
            s_buf[rows] = s
            r_buf[after, rows] = r_buf[par, rows] - alpha * s

        @pl.when(k < ITERS - 1)
        def _():
            for f in range(6):
                rows = slice(f * FACE, (f + 1) * FACE)
                zs_buf[rows] = zq_buf[rows] + beta * zs_buf[rows]
            rows = slice(IF, IF + SLOT)
            zs_buf[rows] = zq_buf[rows] + beta * zs_buf[rows]
            post(after, after, False, alpha)
            launch(after)

        for f in range(6):
            rows = slice(f * FACE, (f + 1) * FACE)
            p = r_buf[par, rows] + beta * p_buf[rows]
            p_buf[rows] = p
            x_buf[rows] = x_buf[rows] + alpha * p
        return alpha, new

    one = jnp.ones((1, LOADS), F32)
    lax.fori_loop(0, ITERS, step, (one, one))

    for f in range(6):
        rows = slice(f * FACE, (f + 1) * FACE)
        x = jnp.transpose(x_buf[rows])
        r = jnp.transpose(r_buf[ITERS % 2, rows])
        mult_ref[:, rows] = -x if f % 2 else x
        out_ref[:, rows] = -r if f % 2 else r


def body(sizes, residual_in, schur, modes, coarse_inv):
    nx, ny, nz = sizes
    direct, relays = gather_plan(nz)
    sends = len(direct) + sum(len(steps) for _, steps in relays)
    plane = nx * ny
    vmem, dma = pltpu.VMEM, pltpu.SemaphoreType.DMA
    field = jax.ShapeDtypeStruct((LOADS, IF), F32)
    mult, resid = pl.pallas_call(
        functools.partial(kernel, sizes),
        out_shape=(field, field),
        in_specs=[pl.BlockSpec(memory_space=pltpu.MemorySpace.HBM)] * 4,
        out_specs=(pl.BlockSpec(memory_space=pltpu.VMEM),) * 2,
        scratch_shapes=[
            vmem((LOADS, IF), F32),
            vmem((IF, IF), F32),
            vmem((MODES, IF), F32),
            vmem((MODES, MODES * nz), F32),
            vmem((SLOT, IF), F32),
            vmem((SLOT, MODES * nz), F32),
            vmem((nz, SLOT, SLOT * nz), F32),
            vmem((SLOT * nz, SLOT * nz), BF16),
            vmem((SLOT * nz, SLOT * nz), BF16),
            vmem((6, SLOT, FACE), F32),
            vmem((IF, 256), BF16),
            vmem((AUG, IF), BF16),
            vmem((AUG, IF), BF16),
            vmem((IF, 2 * LOADS), BF16),
            vmem((2, IF, LOADS), F32),
            vmem((IF, LOADS), F32),
            vmem((IF, LOADS), F32),
            vmem((IF, LOADS), F32),
            vmem((AUG, LOADS), F32),
            vmem((IF, LOADS), F32),
            vmem((AUG, LOADS), F32),
            vmem((AUG, LOADS), F32),
            vmem((2, nz, SLOT, LOADS), F32),
            vmem((2, 4, SLOT, LOADS), F32),
            vmem((nz, SLOT, LOADS), F32),
            vmem((2, LOADS), F32),
            vmem((2, plane, 2, LOADS), F32),
            vmem((2, 6, FACE, LOADS), F32),
            dma((3,)),
            dma((6,)),
            dma((sends,)),
            dma((nz,)),
            dma((6,)),
            dma((6,)),
            dma((sends,)),
            dma((2, nz)),
            dma((6,)),
            dma((2, 6)),
            dma((4,)),
            dma((2, 4)),
            dma((plane - 1,)),
            dma((2, plane - 1)),
        ],
        compiler_params=pltpu.CompilerParams(collective_id=0, has_side_effects=True, vmem_limit_bytes=60 << 20),
    )(residual_in[0, 0, 0], schur[0, 0, 0], modes[0, 0, 0], coarse_inv[0, 0])
    return mult[None, None, None], resid[None, None, None]


def solution(mesh):
    sizes = (mesh.shape["gx"], mesh.shape["gy"], mesh.shape["gz"])
    return jax.shard_map(
        functools.partial(body, sizes),
        mesh=mesh,
        in_specs=(
            P("gx", "gy", "gz", None, None),
            P("gx", "gy", "gz", None, None),
            P("gx", "gy", "gz", None, None),
            P("gx", "gy", "gz", None),
        ),
        out_specs=(P("gx", "gy", "gz", None, None), P("gx", "gy", "gz", None, None)),
        check_vma=False,
    )
```

time: 1010 us -> 123 us (0.12)
  blocking collectives: 797 us -> 0 us
  Pallas kernels: 0 us -> 116 us
  starting transfers between devices: 115 us -> 0 us
  other arithmetic: 33.4 us -> 0 us
  matrix products: 26.4 us -> 0 us
  waiting for transfers between devices: 24.2 us -> 0 us
    psum x4 -> x0, blocking collectives: 609 us -> none  [global_sums(): return lax.psum((first, second), ('gx', 'gy', 'gz'))]
    all_gather x4 -> x0, blocking collectives: 189 us -> none  [operate(): lax.all_gather(loads, 'gz', axis=0, tiled=True)]
    pallas_call x0 -> x1, Pallas kernels: none -> 116 us  [body(): pl.pallas_call(functools.partial(kernel, sizes), out_shape=(field, field)...]
    ppermute x24 -> x0, starting transfers between devices: 115 us -> none  [the longest x12 72.4 us: with_halo(): after = lax.ppermute(initial, axis, down)]
    dot_general x16 -> x0, matrix products: 26.4 us -> none  [the longest x4 13.4 us: operate(): jnp.einsum('rj,ij->ri', u, matrix, precision=lax.Precision.HIGHEST, prefe...]
    ppermute x24 -> x0, waiting for transfers between devices: 24.2 us -> none  [the longest x12 17.4 us: with_halo(): before = lax.ppermute(last, axis, up)]
    unnamed x40 -> x0, other arithmetic: 13.5 us -> none
  transfers between devices with their start and end apart: 24 -> 0, of which waited for: 12 -> 0; matrix products, arithmetic and copies ran while one was open for 0% -> 0% of each run, Pallas kernels for 0% -> 0%
where the time goes in v1:
time: 123 us; the launch traced here: 122 us
  Pallas kernels  116 us (94%)
  local copies, waits for them, and re-layouts  6.16 us (5%)
    pallas_call x1, Pallas kernels, body(): pl.pallas_call(functools.partial(kernel, sizes), out_shape=(field, field)...  116 us
    unnamed x4, local copies, waits for them, and re-layouts  6.16 us

profile of v1, /device:TPU:1, one launch (start us, length us, event | category | flops | bytes accessed | tf_op | source)
XLA Modules:
  0.0 122.5 jit_solution(8238329069226957623)
XLA Ops:
  0.6 1.3 %copy.11 = f32[1,1,6,192]{3,2,1,0:T(8,128)} copy(f32[1,1,6,192]{3,1,2,0:T(1,128)} %param.7) | data formatting | bytes 9216
  1.9 1.3 %copy.10 = f32[1,1,1,6,768]{4,3,2,1,0:T(8,128)} copy(f32[1,1,1,6,768]{4,2,3,1,0:T(1,128)} %param.6) | data formatting | bytes 36864
  3.3 115.7 %shard_map.59 = (f32[128,768]{1,0:T(8,128)}, f32[128,768]{1,0:T(8,128)}) custom-call(f32[128,768]{1,0:T(8,128)} %bitcast.13, f32[768,768]{1,0:T(8,128)} %bitcast.10, f32[6,768]{1,0:T(8,128)} %bitcast.14, f32[6,192]{1,0:T(8,128)} %bitcast.15), custom_call_target="tpu_custom_call" | custom-call | tf_op jit(solution)/shard_map/pallas_call | solution.py:391
  119.0 1.8 %copy.14 = f32[1,1,1,128,768]{4,3,2,1,0:T(8,128)} copy(f32[1,1,1,128,768]{4,3,2,1,0:T(8,128)} %bitcast.12) | data formatting | bytes 786432
  120.7 1.8 %copy.15 = f32[1,1,1,128,768]{4,3,2,1,0:T(8,128)} copy(f32[1,1,1,128,768]{4,3,2,1,0:T(8,128)} %bitcast.11) | data formatting | bytes 786432
